TPU v7x, 128 devices: a whole 4x4x4 slice. The times are simulated.
128 devices in a mesh: row: 16 (over z, x_hi, core), col: 8 (over y, x_lo).
Axes of the slice: x: 4 (x_hi: 2, x_lo: 2; x = x_hi * 2 + x_lo), y: 4, z: 4, core: 2. Of those that a mesh axis runs over, the one named last changes fastest.
Arguments:
- momentum_shards: bfloat16 [6656, 18432], P(('row', 'col')), may hold values from -0.078125 to 0.078125
- shard_starts: int32 [128], replicated, may hold values from 0 to 3568, as said below
Outputs:
- update_shards: bfloat16 [6656, 18432], P(('row', 'col'))
Inputs may be any that keep to these rules, and one draw needn't show every extreme that they name: `shard_starts`: starts never fall and the first is 0; shard d starts within 12 rows of d * 28, and the last one exactly 12 rows after it. Every shard has at most 52 rows and some shard has exactly 52; the 8 shards of one index of row hold at most 248 rows together, and on some index exactly 248.
All inputs are finite; a program needn't handle non-finite values.
Results may differ from a plain program's by a relative error of at most 0.02.
Values may be sent and summed in bfloat16 or wider, within the bound.
A program may use at most 128 MiB of HBM per device.

v0:
```python
import math
import jax
import jax.numpy as jnp
from jax import lax
from jax.sharding import PartitionSpec as P

M = 3584
N = 18432
coef_one = 3.4445
coef_two = -4.775
coef_three = 2.0315


def in_blocks(value, dim, size):
    shape = value.shape
    tiles = value.reshape(*shape[:dim], size, shape[dim] // size, *shape[dim + 1 :])
    return jnp.moveaxis(tiles, dim, 0)


def summed_on_arrival(value, axis, dim):
    size = lax.axis_size(axis)
    tiles = lax.all_to_all(in_blocks(value, dim, size), axis, 0, 0, tiled=True)
    return jnp.sum(tiles.astype(jnp.float32), axis=0)


def laid_out(tiles, dim):
    shape = list(tiles.shape[1:])
    shape[dim] *= tiles.shape[0]
    return jnp.moveaxis(tiles, 0, dim).reshape(shape)


def sent_to_all(value, axis):
    copies = jnp.broadcast_to(value, (lax.axis_size(axis), *value.shape))
    return lax.all_to_all(copies, axis, split_axis=0, concat_axis=0, tiled=True)


def gather_directly(value, axis, dim):
    return laid_out(sent_to_all(value, axis), dim)


def packing(shard_starts, row_block, col_count, shard_rows, window):
    shard_ends = jnp.concatenate([shard_starts[1:], jnp.full((1,), M, jnp.int32)])
    first_starts = lax.dynamic_slice_in_dim(shard_starts, row_block * col_count, col_count)
    last_ends = lax.dynamic_slice_in_dim(shard_ends, row_block * col_count, col_count)
    slot_index = jnp.arange(col_count * shard_rows, dtype=jnp.int32)
    member = slot_index // shard_rows
    offset = slot_index % shard_rows
    pick = member[:, None] == jnp.arange(col_count, dtype=jnp.int32)[None, :]
    shard_begin = jnp.sum(jnp.where(pick, first_starts[None, :], 0), axis=1)
    length = jnp.sum(jnp.where(pick, (last_ends - first_starts)[None, :], 0), axis=1)
    target = shard_begin - first_starts[0] + offset
    is_valid = offset < length
    window_rows = jnp.arange(window, dtype=jnp.int32)
    return ((window_rows[:, None] == target[None, :]) & is_valid[None, :]).astype(jnp.bfloat16)


def body(momentum_shards, shard_starts):
    col_count = lax.axis_size("col")
    row_count = lax.axis_size("row")
    shard_rows = momentum_shards.shape[0]
    mean_rows = M // (row_count * col_count)
    jitter = 4 * (mean_rows // 8)
    window = col_count * mean_rows + 2 * jitter
    packer = packing(shard_starts, lax.axis_index("row"), col_count, shard_rows, window)
    columns = lax.all_to_all(momentum_shards, "col", split_axis=1, concat_axis=0, tiled=True)
    local_tile = jnp.dot(packer, columns, preferred_element_type=jnp.float32).astype(jnp.bfloat16)
    col_panel = lax.all_gather(local_tile, "row", axis=0, tiled=True)
    own_block = summed_on_arrival(
        lax.dot_general(
            col_panel, local_tile, (((1,), (1,)), ((), ())), preferred_element_type=jnp.float32
        ).astype(jnp.bfloat16),
        "col",
        0,
    ).astype(jnp.bfloat16)
    across = lax.all_gather(own_block, "row", axis=1, tiled=True)
    square_own = summed_on_arrival(
        lax.dot_general(
            across, own_block, (((0,), (0,)), ((), ())), preferred_element_type=jnp.float32
        ).astype(jnp.bfloat16),
        "col",
        0,
    )
    poly_own = (coef_two * own_block.astype(jnp.float32) + coef_three * square_own).astype(
        jnp.bfloat16
    )
    poly_block = gather_directly(poly_own, "col", 0)
    mixed_part = lax.dot_general(
        poly_block, col_panel, (((0,), (0,)), ((), ())), preferred_element_type=jnp.float32
    )
    update = (math.sqrt(N) * (coef_one * local_tile.astype(jnp.float32) + mixed_part)).astype(
        jnp.bfloat16
    )
    back_rows = lax.dot_general(
        packer, update, (((0,), (0,)), ((), ())), preferred_element_type=jnp.float32
    ).astype(jnp.bfloat16)
    return lax.all_to_all(back_rows, "col", split_axis=0, concat_axis=1, tiled=True)


def solution(mesh):
    in_specs = (P(("row", "col"), None), P())
    out_specs = P(("row", "col"), None)
    return jax.shard_map(body, mesh=mesh, in_specs=in_specs, out_specs=out_specs, check_vma=False)
```

profile of v0, /device:TPU:0, one launch (start us, length us, event | category | flops | bytes accessed | tf_op | source)
XLA Modules:
  0.0 387.3 jit_solution(3728973360433823546)
XLA Ops:
  6.5 1.9 copy.23
  8.6 1.6 copy.14
  10.2 5.6 %all-to-all-start = ((bf16[52,8,2304]{2,0,1:T(8,128)(2,1)}), bf16[52,8,2304]{2,0,1:T(8,128)(2,1)S(1)}, u32[]{:S(2)}, u32[]{:S(2)}) async-start(bf16[52,8,2304]{2,0,1:T(8,128)(2,1)} %copy.14), calls=%async_computation | async-start | bytes 4128768 | tf_op jit(solution)/shard_map/all_to_all | solution.py:65
  16.3 26.2 %all-to-all-done = bf16[52,8,2304]{2,0,1:T(8,128)(2,1)S(1)} async-done(((bf16[52,8,2304]{2,0,1:T(8,128)(2,1)}), bf16[52,8,2304]{2,0,1:T(8,128)(2,1)S(1)}, u32[]{:S(2)}, u32[]{:S(2)}) %all-to-all-start) | async-done | bytes 1916960 | tf_op jit(solution)/shard_map/all_to_all | solution.py:65
  42.5 1.4 all_to_all.40
  43.9 3.3 convolution_convert_fusion.3
  47.3 116.2 %all-gather.3.cloned.1.call-done = bf16[3968,2304]{1,0:T(8,128)(2,1)} async-done(((bf16[248,2304]{1,0:T(8,128)(2,1)}), bf16[3968,2304]{1,0:T(8,128)(2,1)}) %all-gather.3.cloned.1.call-update) | async-done | bytes 18284560 | tf_op jit(solution)/shard_map/all_gather | solution.py:67
  163.5 12.8 %convolution_convert_fusion.1 = bf16[3968,248]{0,1:T(8,128)(2,1)} fusion(bf16[3968,2304]{1,0:T(8,128)(2,1)} %all-gather.3.cloned.1.call-done, bf16[248,2304]{1,0:T(8,128)(2,1)} %convolution_convert_fusion.3), kind=kOutput, calls=%fused_computation.1 | convolution fusion | flops 4535550976 | bytes 21395456 | tf_op jit(solution)/shard_map/dot_general | solution.py:69
  176.3 5.6 %reshape.48 = bf16[8,496,248]{1,0,2:T(8,128)(2,1)S(1)} reshape(bf16[3968,248]{0,1:T(8,128)(2,1)} %convolution_convert_fusion.1) | data formatting | bytes 3936256 | tf_op jit(solution)/shard_map/reshape | solution.py:16
  181.9 0.7 copy.15
  182.6 30.8 %all_to_all.53 = bf16[8,496,248]{1,2,0:T(8,128)(2,1)S(1)} all-to-all(bf16[8,496,248]{1,2,0:T(8,128)(2,1)S(1)} %copy.15), channel_id=1, replica_groups=mesh['row'=16,'col'=8] {'col'}, dimensions={0} | all-to-all | bytes 3936256 | tf_op jit(solution)/shard_map/all_to_all | solution.py:22
  213.3 1.1 reduce_sum.41
  214.4 51.3 %all-gather.5.cloned.1.call-done = bf16[496,3968]{0,1:T(8,128)(2,1)} async-done(((bf16[496,248]{0,1:T(8,128)(2,1)}), bf16[496,3968]{0,1:T(8,128)(2,1)}) %all-gather.5.cloned.1.call-update) | async-done | bytes 3936272 | tf_op jit(solution)/shard_map/all_gather | solution.py:75
  265.7 4.7 %convolution_convert_fusion = bf16[3968,248]{0,1:T(8,128)(2,1)} fusion(bf16[496,3968]{0,1:T(8,128)(2,1)} %all-gather.5.cloned.1.call-done, bf16[496,248]{0,1:T(8,128)(2,1)} %reduce_sum.41), kind=kOutput, calls=%fused_computation | convolution fusion | flops 977175552 | bytes 6150400 | tf_op jit(solution)/shard_map/dot_general | solution.py:77
  270.5 5.6 %reshape.49 = bf16[8,496,248]{1,0,2:T(8,128)(2,1)S(1)} reshape(bf16[3968,248]{0,1:T(8,128)(2,1)} %convolution_convert_fusion) | data formatting | bytes 3936256 | tf_op jit(solution)/shard_map/reshape | solution.py:16
  276.0 0.7 copy.17
  276.7 30.8 %all_to_all.54 = bf16[8,496,248]{1,2,0:T(8,128)(2,1)S(1)} all-to-all(bf16[8,496,248]{1,2,0:T(8,128)(2,1)S(1)} %copy.17), channel_id=1, replica_groups=mesh['row'=16,'col'=8] {'col'}, dimensions={0} | all-to-all | bytes 3936256 | tf_op jit(solution)/shard_map/all_to_all | solution.py:22
  307.5 0.3 convert_reduce_fusion
  307.8 0.6 copy-done
  308.8 28.6 %all_to_all.55 = bf16[8,496,248]{2,1,0:T(8,128)(2,1)S(1)} all-to-all(bf16[8,496,248]{2,1,0:T(8,128)(2,1)S(1)} %broadcast_in_dim.31), channel_id=1, replica_groups=mesh['row'=16,'col'=8] {'col'}, dimensions={0} | all-to-all | bytes 3936256 | tf_op jit(solution)/shard_map/all_to_all | solution.py:34
  337.4 11.1 %convolution_convert_fusion.2 = bf16[416,2304]{1,0:T(8,128)(2,1)} fusion(s32[416]{0:T(512)S(1)} %subtract_add_fusion, pred[416]{0:T(512)(128)(4,1)S(1)} %fusion.16, bf16[3968,248]{1,0:T(8,128)(2,1)S(1)} %bitcast.27, bf16[3968,2304]{1,0:T(8,128)(2,1)} %all-gather.3.cloned.1.call-done, bf16[248,2304]{1,0:T(8,128)(2,1)S(1)} %copy-done.1), kind=kOutput, calls=%fused_computation.2 | convolution fusion | flops 5013986816 | bytes 23314464 | tf_op jit(solution)/shard_map/dot_general | solution.py:93
  348.5 1.7 all_to_all.44
  350.2 28.1 %all_to_all.56 = bf16[8,52,2304]{2,1,0:T(8,128)(2,1)S(1)} all-to-all(bf16[8,52,2304]{2,1,0:T(8,128)(2,1)S(1)} %all_to_all.44), channel_id=1, replica_groups=mesh['row'=16,'col'=8] {'col'}, dimensions={0} | all-to-all | bytes 3833856 | tf_op jit(solution)/shard_map/all_to_all | solution.py:96
  378.8 1.7 copy.24
  (22 shorter events, 1.4 us)
Async XLA Ops:
  10.2 5.7 %copy-start.2 = (s32[128]{0:T(128)S(1)}, s32[128]{0:T(128)}, u32[]{:S(2)}) copy-start(s32[128]{0:T(128)} %param.3) | copy-start | bytes 1540
  10.2 32.3 %all-to-all-start = ((bf16[52,8,2304]{2,0,1:T(8,128)(2,1)}), bf16[52,8,2304]{2,0,1:T(8,128)(2,1)S(1)}, u32[]{:S(2)}, u32[]{:S(2)}) async-start(bf16[52,8,2304]{2,0,1:T(8,128)(2,1)} %copy.14), calls=%async_computation | async-start | bytes 4128768 | tf_op jit(solution)/shard_map/all_to_all | solution.py:65
  15.9 147.7 %all-gather.3.cloned.1.call-start = ((), (), s32[]{:S(2)}) async-start(), calls=%async_computation.5 | async-start | bytes 19427328 | tf_op jit(solution)/shard_map/all_gather | solution.py:67
  47.3 218.4 %all-gather.5.cloned.1.call-start = ((), (), s32[]{:S(2)}) async-start(), calls=%async_computation.6 | async-start | bytes 4317184 | tf_op jit(solution)/shard_map/all_gather | solution.py:75
  307.5 0.9 copy-start
  308.8 28.6 %copy-start.1 = (bf16[248,2304]{1,0:T(8,128)(2,1)S(1)}, bf16[248,2304]{1,0:T(8,128)(2,1)}, u32[]{:S(2)}) copy-start(bf16[248,2304]{1,0:T(8,128)(2,1)} %convolution_convert_fusion.3) | copy-start | bytes 3428356
Sparse Core Ops, SparseCore 0:
  47.4 116.0 all-gather.2
  214.6 51.1 all-gather.4
where the time goes:
time: 388 us; the launch traced here: 387 us
  waiting for transfers between devices  194 us (50%)
  blocking collectives  118 us (30%)
  matrix products  32 us (8%)
  local copies, waits for them, and re-layouts  22.3 us (6%)
  between operations  13.5 us (3%)
  starting transfers between devices  5.72 us (1%)
    all_gather x1, waiting for transfers between devices, body(): col_panel = lax.all_gather(local_tile, 'row', axis=0, tiled=True)  116 us
    all_to_all x2, blocking collectives, summed_on_arrival(): tiles = lax.all_to_all(in_blocks(value, dim, size), axis, 0, 0, tiled=True)  61.5 us
    all_gather x1, waiting for transfers between devices, body(): across = lax.all_gather(own_block, 'row', axis=1, tiled=True)  51.3 us
    all_to_all x1, blocking collectives, sent_to_all(): return lax.all_to_all(copies, axis, split_axis=0, concat_axis=0, tiled=True)  28.6 us
    all_to_all x1, blocking collectives, body(): lax.all_to_all(back_rows, 'col', split_axis=0, concat_axis=1, tiled=True)  28.1 us
    all_to_all x1, waiting for transfers between devices, body(): lax.all_to_all(momentum_shards, 'col', split_axis=1, concat_axis=0, tiled...  26.2 us
    dot_general x1, matrix products, body(): lax.dot_general(col_panel, local_tile, (((1,), (1,)), ((), ())), preferre...  12.8 us
    reshape x4, local copies, waits for them, and re-layouts, in_blocks(): value.reshape(*shape[:dim], size, shape[dim] // size, *shape[dim + 1:])  12.5 us
  transfers between devices with their start and end apart: 3, of which 3 were waited for; matrix products, arithmetic and copies ran while one was open for 0% of the time, Pallas kernels for 0%

commit v1 on v0

--- a/solution.py
+++ b/solution.py
@@ -72,7 +72,10 @@
         "col",
         0,
     ).astype(jnp.bfloat16)
-    across = lax.all_gather(own_block, "row", axis=1, tiled=True)
+    count = lax.axis_size("row")
+    blocks = jnp.stack([own_block for _ in range(count)])
+    blocks = lax.all_to_all(blocks, "row", split_axis=0, concat_axis=0)
+    across = jnp.concatenate(blocks, axis=1)
     square_own = summed_on_arrival(
         lax.dot_general(
             across, own_block, (((0,), (0,)), ((), ())), preferred_element_type=jnp.float32

time: 388 us -> 384 us (0.990)
  waiting for transfers between devices: 194 us -> 142 us
  blocking collectives: 118 us -> 169 us
    all_to_all x0 -> x1, blocking collectives: none -> 54.2 us  [body(): blocks = lax.all_to_all(blocks, 'row', split_axis=0, concat_axis=0)]
    all_gather x1 -> x0, waiting for transfers between devices: 51.3 us -> none  [body(): across = lax.all_gather(own_block, 'row', axis=1, tiled=True)]
  transfers between devices with their start and end apart: 3 -> 2, of which waited for: 3 -> 2; matrix products, arithmetic and copies ran while one was open for 0% -> 0% of each run, Pallas kernels for 0% -> 0%
where the time goes in v1:
time: 384 us; the launch traced here: 383 us
  blocking collectives  169 us (44%)
  waiting for transfers between devices  142 us (37%)
  matrix products  29.6 us (8%)
  local copies, waits for them, and re-layouts  22 us (6%)
  between operations  13.5 us (4%)
  starting transfers between devices  5.68 us (1%)
    all_gather x1, waiting for transfers between devices, body(): col_panel = lax.all_gather(local_tile, 'row', axis=0, tiled=True)  116 us
    all_to_all x2, blocking collectives, summed_on_arrival(): tiles = lax.all_to_all(in_blocks(value, dim, size), axis, 0, 0, tiled=True)  59.2 us
    all_to_all x1, blocking collectives, body(): blocks = lax.all_to_all(blocks, 'row', split_axis=0, concat_axis=0)  54.2 us
    all_to_all x1, blocking collectives, sent_to_all(): return lax.all_to_all(copies, axis, split_axis=0, concat_axis=0, tiled=True)  27.9 us
    all_to_all x1, blocking collectives, body(): lax.all_to_all(back_rows, 'col', split_axis=0, concat_axis=1, tiled=True)  27.4 us
    all_to_all x1, waiting for transfers between devices, body(): lax.all_to_all(momentum_shards, 'col', split_axis=1, concat_axis=0, tiled...  26.2 us
    dot_general x1, matrix products, body(): lax.dot_general(col_panel, local_tile, (((1,), (1,)), ((), ())), preferre...  12.8 us
    reshape x4, local copies, waits for them, and re-layouts, in_blocks(): value.reshape(*shape[:dim], size, shape[dim] // size, *shape[dim + 1:])  12.5 us
  transfers between devices with their start and end apart: 2, of which 2 were waited for; matrix products, arithmetic and copies ran while one was open for 0% of the time, Pallas kernels for 0%

profile of v1, /device:TPU:0, one launch (start us, length us, event | category | flops | bytes accessed | tf_op | source)
XLA Modules:
  0.0 383.1 jit_solution(17242412043610087692)
XLA Ops:
  6.5 1.9 copy.19
  8.6 1.6 copy.14
  10.2 5.6 %all-to-all-start = ((bf16[52,8,2304]{2,0,1:T(8,128)(2,1)}), bf16[52,8,2304]{2,0,1:T(8,128)(2,1)S(1)}, u32[]{:S(2)}, u32[]{:S(2)}) async-start(bf16[52,8,2304]{2,0,1:T(8,128)(2,1)} %copy.14), calls=%async_computation | async-start | bytes 4128768 | tf_op jit(solution)/shard_map/all_to_all | solution.py:65
  16.3 26.2 %all-to-all-done = bf16[52,8,2304]{2,0,1:T(8,128)(2,1)S(1)} async-done(((bf16[52,8,2304]{2,0,1:T(8,128)(2,1)}), bf16[52,8,2304]{2,0,1:T(8,128)(2,1)S(1)}, u32[]{:S(2)}, u32[]{:S(2)}) %all-to-all-start) | async-done | bytes 1916960 | tf_op jit(solution)/shard_map/all_to_all | solution.py:65
  42.5 1.4 all_to_all.43
  43.9 3.3 convolution_convert_fusion.3
  47.3 116.2 %all-gather.2.cloned.1.call-done = bf16[3968,2304]{1,0:T(8,128)(2,1)} async-done(((bf16[248,2304]{1,0:T(8,128)(2,1)}), bf16[3968,2304]{1,0:T(8,128)(2,1)}) %all-gather.2.cloned.1.call-update) | async-done | bytes 18284560 | tf_op jit(solution)/shard_map/all_gather | solution.py:67
  163.5 12.8 %convolution_convert_fusion.1 = bf16[3968,248]{0,1:T(8,128)(2,1)} fusion(bf16[3968,2304]{1,0:T(8,128)(2,1)} %all-gather.2.cloned.1.call-done, bf16[248,2304]{1,0:T(8,128)(2,1)} %convolution_convert_fusion.3), kind=kOutput, calls=%fused_computation.1 | convolution fusion | flops 4535550976 | bytes 21395456 | tf_op jit(solution)/shard_map/dot_general | solution.py:69
  176.3 5.6 %reshape.56 = bf16[8,496,248]{1,0,2:T(8,128)(2,1)S(1)} reshape(bf16[3968,248]{0,1:T(8,128)(2,1)} %convolution_convert_fusion.1) | data formatting | bytes 3936256 | tf_op jit(solution)/shard_map/reshape | solution.py:16
  181.9 0.7 copy.15
  182.5 30.8 %all_to_all.58 = bf16[8,496,248]{1,2,0:T(8,128)(2,1)S(1)} all-to-all(bf16[8,496,248]{1,2,0:T(8,128)(2,1)S(1)} %copy.15), channel_id=1, replica_groups=mesh['row'=16,'col'=8] {'col'}, dimensions={0} | all-to-all | bytes 3936256 | tf_op jit(solution)/shard_map/all_to_all | solution.py:22
  213.3 0.4 reduce_sum.41
  214.0 54.2 %all_to_all.59 = bf16[16,496,248]{1,2,0:T(8,128)(2,1)S(1)} all-to-all(bf16[16,496,248]{1,2,0:T(8,128)(2,1)S(1)} %stack.2), channel_id=1, replica_groups=mesh['row'=16,'col'=8] {'row'}, dimensions={0} | all-to-all | bytes 7872512 | tf_op jit(solution)/shard_map/all_to_all | solution.py:77
  268.2 2.6 convolution_convert_fusion
  270.8 5.6 %reshape.59 = bf16[8,496,248]{1,0,2:T(8,128)(2,1)S(1)} reshape(bf16[3968,248]{0,1:T(8,128)(2,1)} %convolution_convert_fusion) | data formatting | bytes 3936256 | tf_op jit(solution)/shard_map/reshape | solution.py:16
  276.4 0.7 copy.16
  277.0 28.4 %all_to_all.60 = bf16[8,496,248]{1,2,0:T(8,128)(2,1)S(1)} all-to-all(bf16[8,496,248]{1,2,0:T(8,128)(2,1)S(1)} %copy.16), channel_id=1, replica_groups=mesh['row'=16,'col'=8] {'col'}, dimensions={0} | all-to-all | bytes 3936256 | tf_op jit(solution)/shard_map/all_to_all | solution.py:22
  305.4 0.3 convert_reduce_fusion
  306.1 27.9 %all_to_all.61 = bf16[8,496,248]{2,1,0:T(8,128)(2,1)S(1)} all-to-all(bf16[8,496,248]{2,1,0:T(8,128)(2,1)S(1)} %broadcast_in_dim.31), channel_id=1, replica_groups=mesh['row'=16,'col'=8] {'col'}, dimensions={0} | all-to-all | bytes 3936256 | tf_op jit(solution)/shard_map/all_to_all | solution.py:34
  334.1 11.0 %convolution_convert_fusion.2 = bf16[416,2304]{1,0:T(8,128)(2,1)} fusion(s32[416]{0:T(512)S(1)} %subtract_add_fusion, pred[416]{0:T(512)(128)(4,1)S(1)} %fusion.16, bf16[3968,248]{1,0:T(8,128)(2,1)S(1)} %bitcast.31, bf16[3968,2304]{1,0:T(8,128)(2,1)} %all-gather.2.cloned.1.call-done, bf16[248,2304]{1,0:T(8,128)(2,1)S(1)} %copy-done), kind=kOutput, calls=%fused_computation.2 | convolution fusion | flops 5013986816 | bytes 23314464 | tf_op jit(solution)/shard_map/dot_general | solution.py:96
  345.1 1.7 all_to_all.48
  346.8 27.4 %all_to_all.62 = bf16[8,52,2304]{2,1,0:T(8,128)(2,1)S(1)} all-to-all(bf16[8,52,2304]{2,1,0:T(8,128)(2,1)S(1)} %all_to_all.48), channel_id=1, replica_groups=mesh['row'=16,'col'=8] {'col'}, dimensions={0} | all-to-all | bytes 3833856 | tf_op jit(solution)/shard_map/all_to_all | solution.py:99
  374.2 0.3 copy.18
  374.6 1.7 copy.20
  (19 shorter events, 1.3 us)
Async XLA Ops:
  10.2 5.7 %copy-start.1 = (s32[128]{0:T(128)S(1)}, s32[128]{0:T(128)}, u32[]{:S(2)}) copy-start(s32[128]{0:T(128)} %param.3) | copy-start | bytes 1540
  10.2 32.3 %all-to-all-start = ((bf16[52,8,2304]{2,0,1:T(8,128)(2,1)}), bf16[52,8,2304]{2,0,1:T(8,128)(2,1)S(1)}, u32[]{:S(2)}, u32[]{:S(2)}) async-start(bf16[52,8,2304]{2,0,1:T(8,128)(2,1)} %copy.14), calls=%async_computation | async-start | bytes 4128768 | tf_op jit(solution)/shard_map/all_to_all | solution.py:65
  15.9 147.6 %all-gather.2.cloned.1.call-start = ((), (), s32[]{:S(2)}) async-start(), calls=%async_computation.6 | async-start | bytes 19427328 | tf_op jit(solution)/shard_map/all_gather | solution.py:67
  306.1 28.0 %copy-start = (bf16[248,2304]{1,0:T(8,128)(2,1)S(1)}, bf16[248,2304]{1,0:T(8,128)(2,1)}, u32[]{:S(2)}) copy-start(bf16[248,2304]{1,0:T(8,128)(2,1)} %convolution_convert_fusion.3) | copy-start | bytes 3428356
Sparse Core Ops, SparseCore 0:
  47.4 116.0 all-gather.1
